TPU v7x, 256 devices: a whole 4x4x8 slice. The times are simulated.
256 devices in a mesh: src: 2 (over y_lo), tx: 8 (over y_hi, x), ty: 16 (over z, core).
Axes of the slice: x: 4, y: 4 (y_hi: 2, y_lo: 2; y = y_hi * 2 + y_lo), z: 8, core: 2. Of those that a mesh axis runs over, the one named last changes fastest.
Arguments:
- orders: float32 [8, 2, 512, 512], P('src', None, 'tx', 'ty'), may hold values from -0.00390625 to 0.00390625
- offsets: int32 [8, 2], P('src'), may hold values from -8 to 7
- material: int32 [6, 2048, 2048], P(None, 'tx', 'ty'), may hold values from 0 to 3
- e_field: float32 [3, 6, 2048, 2048], P(None, None, 'tx', 'ty'), may hold values from -6 to 6
- h_field: float32 [3, 6, 2048, 2048], P(None, None, 'tx', 'ty'), may hold values from -6 to 6
Outputs:
- e_out: float32 [3, 6, 2048, 2048], P(None, None, 'tx', 'ty')
- h_out: float32 [3, 6, 2048, 2048], P(None, None, 'tx', 'ty')
All inputs are finite; a program needn't handle non-finite values.
Results may differ from a plain program's by a relative error of at most 0.0003.
Values sent between devices are 32-bit elements; how exact they have to be, the bound alone decides.
A program may use at most 128 MiB of HBM per device.

v0:
```python
import math
import jax
import jax.numpy as jnp
from jax import lax
from jax.sharding import PartitionSpec as P

STEPS = 4
ZINJ = 1
COURANT = 0.5
OMEGA = 0.7
PERMITTIVITY = (1.0, 2.6, 11.9, 2.1)
PREC = lax.Precision.HIGH
SPLIT = 32


def passed_along(block, axis, distance):
    devices = range(lax.axis_size(axis))
    route = [((i - distance) % len(devices), i) for i in devices]
    return lax.ppermute(block, axis, route)


def phase_tables(freqs, positions, length):
    product = jnp.mod(freqs[:, None] * positions[None, :], length)
    angle = product.astype(jnp.float32) * (2.0 * math.pi / length)
    return (jnp.cos(angle), jnp.sin(angle))


def base_tables(orders_n, positions, length):
    hi = jnp.arange(orders_n // SPLIT, dtype=jnp.int32) * SPLIT
    lo = jnp.arange(SPLIT, dtype=jnp.int32) - orders_n // 2
    c1, s1 = phase_tables(hi, positions, length)
    c2, s2 = phase_tables(lo, positions, length)
    cos_t = c1[:, None, :] * c2[None, :, :] - s1[:, None, :] * s2[None, :, :]
    sin_t = s1[:, None, :] * c2[None, :, :] + c1[:, None, :] * s2[None, :, :]
    return (cos_t.reshape(orders_n, -1), sin_t.reshape(orders_n, -1))


def cell_coefficient(material):
    total = jnp.zeros(material.shape, jnp.float32)
    for number in range(len(PERMITTIVITY)):
        total = total + jnp.where(material == number, COURANT / PERMITTIVITY[number], 0.0)
    return total


def fwd(field, axis):
    if axis == 0:
        zero = jnp.zeros((1,) + field.shape[1:], jnp.float32)
        return jnp.concatenate([field[1:], zero], 0) - field
    return jnp.roll(field, -1, axis) - field


def bwd(field, axis):
    if axis == 0:
        zero = jnp.zeros((1,) + field.shape[1:], jnp.float32)
        return field - jnp.concatenate([zero, field[:-1]], 0)
    return field - jnp.roll(field, 1, axis)


def injection_plane(orders, offsets, cells_x, cells_y):
    points, _, rows_kx, cols_ky = orders.shape
    n_tx = lax.axis_size("tx")
    n_ty = lax.axis_size("ty")
    full_x = cells_x * n_tx
    full_y = cells_y * n_ty
    mx = rows_kx * n_tx
    my = cols_ky * n_ty
    amp = lax.all_gather(orders, "ty", axis=3, tiled=True)
    a_re = amp[:, 0]
    a_im = amp[:, 1]
    y_pos = lax.axis_index("ty") * cells_y + jnp.arange(cells_y, dtype=jnp.int32)
    by_c, by_s = base_tables(my, y_pos, full_y)
    sy_c, sy_s = phase_tables(offsets[:, 1], y_pos, full_y)
    m_re = jnp.einsum("pkj,jy->pky", a_re, by_c, precision=PREC) - jnp.einsum(
        "pkj,jy->pky", a_im, by_s, precision=PREC
    )
    m_im = jnp.einsum("pkj,jy->pky", a_re, by_s, precision=PREC) + jnp.einsum(
        "pkj,jy->pky", a_im, by_c, precision=PREC
    )
    sy_c = sy_c[:, None, :]
    sy_s = sy_s[:, None, :]
    inner = jnp.stack([m_re * sy_c - m_im * sy_s, m_re * sy_s + m_im * sy_c], 1)
    inner = lax.all_gather(inner, "tx", axis=2, tiled=True)
    i_re = inner[:, 0]
    i_im = inner[:, 1]
    x_pos = lax.axis_index("tx") * cells_x + jnp.arange(cells_x, dtype=jnp.int32)
    bx_c, bx_s = base_tables(mx, x_pos, full_x)
    sx_c, sx_s = phase_tables(offsets[:, 0], x_pos, full_x)
    q_re = jnp.einsum("kx,pky->pxy", bx_c, i_re, precision=PREC) - jnp.einsum(
        "kx,pky->pxy", bx_s, i_im, precision=PREC
    )
    q_im = jnp.einsum("kx,pky->pxy", bx_c, i_im, precision=PREC) + jnp.einsum(
        "kx,pky->pxy", bx_s, i_re, precision=PREC
    )
    sx_c = sx_c[:, :, None]
    sx_s = sx_s[:, :, None]
    plane = jnp.stack(
        [jnp.sum(q_re * sx_c - q_im * sx_s, 0), jnp.sum(q_re * sx_s + q_im * sx_c, 0)]
    )
    return lax.psum(plane, "src")


def with_halo(stack, depth):
    ahead = passed_along(stack[:, :depth], "tx", -1)
    behind = passed_along(stack[:, -depth:], "tx", 1)
    stack = jnp.concatenate([stack, ahead, behind], 1)
    ahead = passed_along(jnp.swapaxes(stack[:, :, :depth], 1, 2), "ty", -1)
    behind = passed_along(jnp.swapaxes(stack[:, :, -depth:], 1, 2), "ty", 1)
    return jnp.concatenate([stack, jnp.swapaxes(ahead, 1, 2), jnp.swapaxes(behind, 1, 2)], 2)


def per_device(orders, offsets, material, e_field, h_field):
    layers, cells_x, cells_y = material.shape
    plane = injection_plane(orders, offsets, cells_x, cells_y)
    coefficient = cell_coefficient(material)
    stack = jnp.concatenate(
        [
            e_field.reshape(3 * layers, cells_x, cells_y),
            h_field.reshape(3 * layers, cells_x, cells_y),
            coefficient,
            plane,
        ],
        0,
    )
    ext = with_halo(stack, STEPS)
    n = 3 * layers
    e_x, e_y, e_z = (ext[i * layers : (i + 1) * layers] for i in range(3))
    h_x, h_y, h_z = (ext[n + i * layers : n + (i + 1) * layers] for i in range(3))
    coefficient = ext[2 * n : 2 * n + layers]
    plane_re = ext[2 * n + layers]
    plane_im = ext[2 * n + layers + 1]
    for step in range(STEPS):
        h_x = h_x - COURANT * (fwd(e_z, 2) - fwd(e_y, 0))
        h_y = h_y - COURANT * (fwd(e_x, 0) - fwd(e_z, 1))
        h_z = h_z - COURANT * (fwd(e_y, 1) - fwd(e_x, 2))
        e_x = e_x + coefficient * (bwd(h_z, 2) - bwd(h_y, 0))
        e_y = e_y + coefficient * (bwd(h_x, 0) - bwd(h_z, 1))
        e_z = e_z + coefficient * (bwd(h_y, 1) - bwd(h_x, 2))
        cosine = math.cos(OMEGA * (step + 1))
        sine = math.sin(OMEGA * (step + 1))
        e_x = e_x.at[ZINJ].add(COURANT * (cosine * plane_re - sine * plane_im))
        e_y = e_y.at[ZINJ].add(COURANT * (sine * plane_re + cosine * plane_im))
    crop = lambda f: f[:, :cells_x, :cells_y]
    return (
        jnp.stack([crop(e_x), crop(e_y), crop(e_z)]),
        jnp.stack([crop(h_x), crop(h_y), crop(h_z)]),
    )


def solution(mesh):
    in_specs = (
        P("src", None, "tx", "ty"),
        P("src", None),
        P(None, "tx", "ty"),
        P(None, None, "tx", "ty"),
        P(None, None, "tx", "ty"),
    )
    out_specs = (P(None, None, "tx", "ty"), P(None, None, "tx", "ty"))
    return jax.shard_map(
        per_device, mesh=mesh, in_specs=in_specs, out_specs=out_specs, check_vma=False
    )
```

profile of v0, /device:TPU:1, one launch (start us, length us, event | category | flops | bytes accessed | tf_op | source)
XLA Modules:
  0.0 297.1 jit_solution(6683656501134292388)
XLA Ops:
  7.2 1.6 copy.27
  10.9 43.5 %all-gather.3.cloned.1.call-done = f32[4,2,64,512]{2,0,1,3:T(4,128)} async-done(((f32[4,2,64,32]{2,0,1,3:T(4,128)}), f32[4,2,64,512]{2,0,1,3:T(4,128)}) %all-gather.3.cloned.1.call-update) | async-done | bytes 1048592 | tf_op jit(solution)/shard_map/all_gather | solution.py:67
  54.4 1.7 fusion.128
  60.0 56.0 %all-gather.5.cloned.1.call-done = f32[4,2,512,128]{3,2,0,1:T(8,128)} async-done(((f32[4,2,64,128]{3,2,0,1:T(8,128)}), f32[4,2,512,128]{3,2,0,1:T(8,128)}) %all-gather.5.cloned.1.call-update) | async-done | bytes 2097168 | tf_op jit(solution)/shard_map/all_gather | solution.py:82
  116.0 2.4 fusion.75
  118.4 1.0 fusion.74
  119.4 1.0 convolution_subtract_fusion
  120.4 1.0 subtract_reduce_fusion
  122.2 1.5 select_add_fusion
  123.7 33.4 %all-reduce.18.cloned.1.call-done = f32[2,256,128]{1,2,0:T(8,128)} async-done(((f32[2,256,128]{1,2,0:T(8,128)}), f32[2,256,128]{1,2,0:T(8,128)}) %all-reduce.18.cloned.1.call-update) | async-done | bytes 262160 | tf_op jit(solution)/shard_map/psum | solution.py:99
  157.0 1.1 copy.34
  158.1 1.1 pad_maximum_fusion.21
  159.3 4.6 %collective-permute-start = (f32[44,4,128]{2,1,0:T(4,128)S(1)}, f32[44,4,128]{2,1,0:T(4,128)S(1)}, u32[]{:S(2)}, u32[]{:S(2)}) collective-permute-start(f32[44,4,128]{2,1,0:T(4,128)S(1)} %get-tuple-element.134), channel_id=1, source_target_pairs={{16,0},{32,16},{48,32},{64,48},{80,64},{96,80},{112,96},{0,112},{1... | collective-permute-start | bytes 270344 | tf_op jit(solution)/shard_map/ppermute | solution.py:19
  163.9 1.6 collective-permute-done
  165.5 5.4 %collective-permute-done.1 = f32[44,4,128]{2,1,0:T(4,128)S(1)} collective-permute-done((f32[44,4,128]{2,1,0:T(4,128)S(1)}, f32[44,4,128]{2,1,0:T(4,128)S(1)}, u32[]{:S(2)}, u32[]{:S(2)}) %collective-permute-start.1) | collective-permute-done | bytes 90144 | tf_op jit(solution)/shard_map/ppermute | solution.py:19
  170.9 2.1 pad_maximum_fusion.1
  173.0 6.2 %slice_bitcast_fusion.1 = (f32[44,4,264]{1,2,0:T(8,128)}, f32[44,4,264]{1,2,0:T(8,128)}) fusion(f32[44,264,128]{2,1,0:T(8,128)S(1)} %pad_maximum_fusion.1), kind=kLoop, calls=%fused_computation.2 | loop fusion | bytes 743424 | tf_op jit(solution)/shard_map/transpose | solution.py:106
  179.2 5.5 %copy.35 = f32[44,4,264]{2,1,0:T(4,128)} copy(f32[44,4,264]{1,2,0:T(8,128)} %get-tuple-element.132) | data formatting | bytes 371712 | tf_op jit(solution)/shard_map/transpose | solution.py:106
  184.8 2.6 collective-permute-start.2
  187.3 5.5 %copy.37 = f32[44,4,264]{2,1,0:T(4,128)} copy(f32[44,4,264]{1,2,0:T(8,128)} %get-tuple-element.133) | data formatting | bytes 371712 | tf_op jit(solution)/shard_map/transpose | solution.py:107
  192.8 1.2 collective-permute-start.3
  194.0 4.8 %copy.36 = f32[44,4,264]{1,2,0:T(8,128)} copy(f32[44,4,264]{2,1,0:T(4,128)} %collective-permute-done.2) | data formatting | bytes 371712 | tf_op jit(solution)/shard_map/ppermute | solution.py:19
  198.8 4.9 %copy.38 = f32[44,4,264]{1,2,0:T(8,128)} copy(f32[44,4,264]{2,1,0:T(4,128)} %collective-permute-done.3) | data formatting | bytes 371712 | tf_op jit(solution)/shard_map/ppermute | solution.py:19
  203.7 7.5 %pad_maximum_fusion = f32[44,264,136]{2,1,0:T(8,128)S(1)} fusion(f32[44,264,4]{2,1,0:T(8,128)} %bitcast.125, f32[44,264,4]{2,1,0:T(8,128)} %bitcast.124, f32[44,4,128]{2,1,0:T(4,128)} %copy-done.15, f32[44,4,128]{2,1,0:T(4,128)S(1)} %collective-permute-done, f32[2,256,128]{2,1,0:T(8,128)S(1)} %copy.34, f32[6,256,128]{2,1,0:T(8,128)S(1)} %select_add_fusion, ...), kind=kLoop, calls=%fused_computation | loop fusion | flops 11058432 | bytes 12638208 | tf_op jit(solution)/shard_map/concatenate | solution.py:108
  211.4 0.9 fusion.124
  212.3 2.5 copy-done.3
  215.6 1.2 slice.667
  217.1 2.7 fusion.9
  221.5 2.3 fusion.17
  223.8 1.0 slice.674
  225.1 1.0 slice.661
  226.0 1.2 slice.664
  227.3 1.6 slice.660
  229.0 1.7 slice.673
  230.6 1.3 slice.669
  232.6 4.1 %fusion.20 = (f32[6,264,136]{2,1,0:T(8,128)S(1)}, f32[6,264,136]{2,1,0:T(8,128)S(1)}, f32[6,264,136]{2,1,0:T(8,128)S(1)}) fusion(f32[6,264,136]{2,1,0:T(8,128)S(1)} %get-tuple-element.122, f32[6,264,136]{2,1,0:T(8,128)S(1)} %get-tuple-element.120, f32[6,1,136]{2,1,0:T(1,128)S(1)} %slice.659, f32[6,263,136]{2,1,0:T(8,128)S(1)} %slice.658, ...), kind=kLoop, calls=%fused_computation.42 | loop fusion | flops 4093056 | bytes 12638208 | tf_op jit(solution)/shard_map/sub | solution.py:134
  236.8 1.2 slice.662
  238.0 1.2 slice.671
  239.1 1.2 slice.689
  240.3 1.2 slice.676
  241.5 3.5 %fusion.35 = (f32[6,264,136]{2,1,0:T(8,128)S(1)}, f32[6,264,136]{2,1,0:T(8,128)S(1)}, f32[6,264,136]{2,1,0:T(8,128)S(1)}) fusion(f32[6,264,136]{2,1,0:T(8,128)S(1)} %get-tuple-element.120, f32[6,264,136]{2,1,0:T(8,128)S(1)} %get-tuple-element.147, f32[6,263,136]{2,1,0:T(8,128)S(1)} %bitcast.108, f32[6,1,136]{2,1,0:T(1,128)S(1)} %slice.677, ...), kind=kLoop, calls=%fused_computation.64 | loop fusion | flops 4093056 | bytes 13499904 | tf_op jit(solution)/shard_map/add | solution.py:136
  245.0 1.0 slice.696
  246.2 1.0 slice.683
  247.2 1.2 slice.686
  248.5 1.6 slice.682
  250.2 1.7 slice.695
  251.8 1.3 slice.691
  253.1 4.1 %fusion.38 = (f32[6,264,136]{2,1,0:T(8,128)S(1)}, f32[6,264,136]{2,1,0:T(8,128)S(1)}, f32[6,264,136]{2,1,0:T(8,128)S(1)}) fusion(f32[6,264,136]{2,1,0:T(8,128)S(1)} %get-tuple-element.147, f32[6,264,136]{2,1,0:T(8,128)S(1)} %get-tuple-element.118, f32[6,1,136]{2,1,0:T(1,128)S(1)} %slice.681, f32[6,263,136]{2,1,0:T(8,128)S(1)} %slice.680, ...), kind=kLoop, calls=%fused_computation.68 | loop fusion | flops 4093056 | bytes 12638208 | tf_op jit(solution)/shard_map/sub | solution.py:134
  257.3 1.4 slice.684
  258.7 1.2 slice.693
  259.9 1.2 slice.711
  261.1 1.2 slice.698
  263.0 3.5 %fusion.53 = (f32[6,264,136]{2,1,0:T(8,128)S(1)}, f32[6,264,136]{2,1,0:T(8,128)S(1)}, f32[6,264,136]{2,1,0:T(8,128)S(1)}) fusion(f32[6,264,136]{2,1,0:T(8,128)S(1)} %get-tuple-element.118, f32[6,264,136]{2,1,0:T(8,128)S(1)} %get-tuple-element.144, f32[6,263,136]{2,1,0:T(8,128)S(1)} %bitcast.110, f32[6,1,136]{2,1,0:T(1,128)S(1)} %slice.699, ...), kind=kLoop, calls=%fused_computation.90 | loop fusion | flops 4093056 | bytes 13499904 | tf_op jit(solution)/shard_map/add | solution.py:136
  268.3 1.3 copy-done.6
  269.6 2.3 fusion.56
  271.9 1.4 slice.706
  273.4 1.2 slice.728
  274.6 1.2 slice.721
  276.5 5.5 %fusion.59 = (f32[6,264,136]{2,1,0:T(8,128)}, f32[6,264,136]{2,1,0:T(8,128)}, f32[6,264,136]{2,1,0:T(8,128)}) fusion(f32[6,264,136]{2,1,0:T(8,128)S(1)} %get-tuple-element.117, f32[6,264,136]{2,1,0:T(8,128)S(1)} %get-tuple-element.141, f32[6,264,135]{2,1,0:T(8,128)S(1)} %bitcast.117, f32[6,264,1]{2,1,0:T(8,128)} %slice.706, ...), kind=kLoop, calls=%fused_computation.99 | loop fusion | flops 2585088 | bytes 10914816 | tf_op jit(solution)/shard_map/add | solution.py:135
  282.0 2.1 fusion.87
  284.1 1.6 slice_bitcast_fusion.9
  285.7 1.7 slice_bitcast_fusion.11
  287.4 1.6 pad_maximum_fusion.3
  289.0 1.6 pad_maximum_fusion.2
  (99 shorter events, 14.5 us)
Async XLA Ops:
  7.2 47.2 %all-gather.3.cloned.1.call-start = ((), (), s32[]{:S(2)}) async-start(), calls=%async_computation | async-start | bytes 2228224 | tf_op jit(solution)/shard_map/all_gather | solution.py:67
  8.9 107.1 %all-gather.5.cloned.1.call-start = ((), (), s32[]{:S(2)}) async-start(), calls=%async_computation.1 | async-start | bytes 2359296 | tf_op jit(solution)/shard_map/all_gather | solution.py:82
  56.4 1.0 copy-start.14
  59.3 97.8 %all-reduce.18.cloned.1.call-start = ((), (), s32[]{:S(2)}) async-start(), calls=%async_computation.2 | async-start | bytes 524288 | tf_op jit(solution)/shard_map/psum | solution.py:99
  116.0 2.4 copy-start.11
  121.5 36.7 %copy-start.1 = (f32[3,6,256,128]{3,2,1,0:T(8,128)S(1)}, f32[3,6,256,128]{3,2,1,0:T(8,128)}, u32[]{:S(2)}) copy-start(f32[3,6,256,128]{3,2,1,0:T(8,128)} %param.25) | copy-start | bytes 7077892
  158.1 12.8 %copy-start.2 = (f32[3,6,256,128]{3,2,1,0:T(8,128)S(1)}, f32[3,6,256,128]{3,2,1,0:T(8,128)}, u32[]{:S(2)}) copy-start(f32[3,6,256,128]{3,2,1,0:T(8,128)} %param.24) | copy-start | bytes 7077892
  159.3 6.2 %collective-permute-start = (f32[44,4,128]{2,1,0:T(4,128)S(1)}, f32[44,4,128]{2,1,0:T(4,128)S(1)}, u32[]{:S(2)}, u32[]{:S(2)}) collective-permute-start(f32[44,4,128]{2,1,0:T(4,128)S(1)} %get-tuple-element.134), channel_id=1, source_target_pairs={{16,0},{32,16},{48,32},{64,48},{80,64},{96,80},{112,96},{0,112},{1... | collective-permute-start | bytes 270344 | tf_op jit(solution)/shard_map/ppermute | solution.py:19
  163.9 7.0 %collective-permute-start.1 = (f32[44,4,128]{2,1,0:T(4,128)S(1)}, f32[44,4,128]{2,1,0:T(4,128)S(1)}, u32[]{:S(2)}, u32[]{:S(2)}) collective-permute-start(f32[44,4,128]{2,1,0:T(4,128)S(1)} %get-tuple-element.135), channel_id=1, source_target_pairs={{112,0},{0,16},{16,32},{32,48},{48,64},{64,80},{80,96},{96,112},{1... | collective-permute-start | bytes 270344 | tf_op jit(solution)/shard_map/ppermute | solution.py:19
  170.9 2.1 copy-start.15
  184.8 9.2 %collective-permute-start.2 = (f32[44,4,264]{2,1,0:T(4,128)}, f32[44,4,264]{2,1,0:T(4,128)}, u32[]{:S(2)}, u32[]{:S(2)}) collective-permute-start(f32[44,4,264]{2,1,0:T(4,128)} %copy.35), channel_id=1, source_target_pairs={{1,0},{2,1},{3,2},{4,3},{5,4},{6,5},{7,6},{8,7},{9,8},{10,9},{11,1... | collective-permute-start | bytes 557576 | tf_op jit(solution)/shard_map/ppermute | solution.py:19
  192.8 6.0 %collective-permute-start.3 = (f32[44,4,264]{2,1,0:T(4,128)}, f32[44,4,264]{2,1,0:T(4,128)}, u32[]{:S(2)}, u32[]{:S(2)}) collective-permute-start(f32[44,4,264]{2,1,0:T(4,128)} %copy.37), channel_id=1, source_target_pairs={{15,0},{0,1},{1,2},{2,3},{3,4},{4,5},{5,6},{6,7},{7,8},{8,9},{9,10... | collective-permute-start | bytes 557576 | tf_op jit(solution)/shard_map/ppermute | solution.py:19
  211.2 55.4 %copy-start = (f32[44,264,136]{2,1,0:T(8,128)}, f32[44,264,136]{2,1,0:T(8,128)S(1)}, u32[]{:S(2)}) copy-start(f32[44,264,136]{2,1,0:T(8,128)S(1)} %pad_maximum_fusion) | copy-start | bytes 18957316
  211.4 3.4 %copy-start.3 = (f32[3,6,256,128]{3,2,1,0:T(8,128)S(1)}, f32[3,6,256,128]{3,2,1,0:T(8,128)}, u32[]{:S(2)}) copy-start(f32[3,6,256,128]{3,2,1,0:T(8,128)} %param.24) | copy-start | bytes 7077892
  211.4 3.4 %copy-start.16 = (f32[44,4,128]{2,1,0:T(4,128)S(1)}, f32[44,4,128]{2,1,0:T(4,128)}, u32[]{:S(2)}) copy-start(f32[44,4,128]{2,1,0:T(4,128)} %copy-done.15) | copy-start | bytes 270340
  219.8 1.2 copy-start.7
  220.1 1.4 copy-start.13
  230.6 2.0 copy-start.8
  257.3 2.7 copy-start.4
  261.1 1.9 copy-start.5
  268.1 1.4 copy-start.6
  271.9 1.5 copy-start.9
  274.6 1.9 copy-start.10
  284.1 1.6 copy-start.12
Sparse Core Ops, SparseCore 0:
  10.4 43.9 all-gather.2
  59.4 56.5 all-gather.4
  122.3 34.6 all-reduce.17
where the time goes:
time: 298 us; the launch traced here: 297 us
  waiting for transfers between devices  140 us (47%)
  local copies, waits for them, and re-layouts  75.9 us (25%)
  other arithmetic  51.6 us (17%)
  between operations  14.4 us (5%)
  starting transfers between devices  8.49 us (3%)
  matrix products  6.93 us (2%)
    all_gather x1, waiting for transfers between devices, injection_plane(): inner = lax.all_gather(inner, 'tx', axis=2, tiled=True)  56 us
    all_gather x1, waiting for transfers between devices, injection_plane(): amp = lax.all_gather(orders, 'ty', axis=3, tiled=True)  43.5 us
    psum x1, waiting for transfers between devices, injection_plane(): return lax.psum(plane, 'src')  33.4 us
    slice x27, local copies, waits for them, and re-layouts, fwd(): return jnp.roll(field, -1, axis) - field  15.9 us
    sub x4, other arithmetic, per_device(): h_z = h_z - COURANT * (fwd(e_y, 1) - fwd(e_x, 2))  13.2 us
    transpose x2, local copies, waits for them, and re-layouts, with_halo(): ahead = passed_along(jnp.swapaxes(stack[:, :, :depth], 1, 2), 'ty', -1)  11.7 us
    unnamed x37, local copies, waits for them, and re-layouts  9.9 us
    ppermute x2, local copies, waits for them, and re-layouts, passed_along(): return lax.ppermute(block, axis, route)  9.72 us
  transfers between devices with their start and end apart: 7, of which 5 were waited for; matrix products, arithmetic and copies ran while one was open for 5% of the time, Pallas kernels for 0%

commit v1 on v0

--- a/solution.py
+++ b/solution.py
@@ -11,6 +11,13 @@
 PERMITTIVITY = (1.0, 2.6, 11.9, 2.1)
 PREC = lax.Precision.HIGH
 SPLIT = 32
+
+
+def exchange_gather(x, mesh_axis, along):
+    peers = lax.axis_size(mesh_axis)
+    blocks = jnp.stack([x for _ in range(peers)])
+    blocks = lax.all_to_all(blocks, mesh_axis, split_axis=0, concat_axis=0)
+    return jnp.concatenate(blocks, axis=along)
 
 
 def passed_along(block, axis, distance):
@@ -79,7 +86,7 @@
     sy_c = sy_c[:, None, :]
     sy_s = sy_s[:, None, :]
     inner = jnp.stack([m_re * sy_c - m_im * sy_s, m_re * sy_s + m_im * sy_c], 1)
-    inner = lax.all_gather(inner, "tx", axis=2, tiled=True)
+    inner = exchange_gather(inner, "tx", 2)
     i_re = inner[:, 0]
     i_im = inner[:, 1]
     x_pos = lax.axis_index("tx") * cells_x + jnp.arange(cells_x, dtype=jnp.int32)

time: 298 us -> 276 us (0.926)
  waiting for transfers between devices: 140 us -> 111 us
  starting transfers between devices: 8.49 us -> 14.9 us
    all_gather x1 -> x0, waiting for transfers between devices: 56 us -> none  [injection_plane(): inner = lax.all_gather(inner, 'tx', axis=2, tiled=True)]
    all_to_all x0 -> x1, waiting for transfers between devices: none -> 27.9 us  [exchange_gather(): blocks = lax.all_to_all(blocks, mesh_axis, split_axis=0, concat_axis=0)]
    all_to_all x0 -> x1, starting transfers between devices: none -> 6.42 us  [exchange_gather(): blocks = lax.all_to_all(blocks, mesh_axis, split_axis=0, concat_axis=0)]
    unnamed x37 -> x35, local copies, waits for them, and re-layouts: 9.9 us -> 9.92 us
where the time goes in v1:
time: 276 us; the launch traced here: 275 us
  waiting for transfers between devices  111 us (40%)
  local copies, waits for them, and re-layouts  77.7 us (28%)
  other arithmetic  50.9 us (18%)
  starting transfers between devices  14.9 us (5%)
  between operations  14.7 us (5%)
  matrix products  5.65 us (2%)
    all_gather x1, waiting for transfers between devices, injection_plane(): amp = lax.all_gather(orders, 'ty', axis=3, tiled=True)  43.5 us
    psum x1, waiting for transfers between devices, injection_plane(): return lax.psum(plane, 'src')  32.6 us
    all_to_all x1, waiting for transfers between devices, exchange_gather(): blocks = lax.all_to_all(blocks, mesh_axis, split_axis=0, concat_axis=0)  27.9 us
    slice x27, local copies, waits for them, and re-layouts, fwd(): return jnp.roll(field, -1, axis) - field  15.8 us
    sub x4, other arithmetic, per_device(): h_z = h_z - COURANT * (fwd(e_y, 1) - fwd(e_x, 2))  13.2 us
    transpose x2, local copies, waits for them, and re-layouts, with_halo(): ahead = passed_along(jnp.swapaxes(stack[:, :, :depth], 1, 2), 'ty', -1)  11.7 us
    unnamed x35, local copies, waits for them, and re-layouts  9.92 us
    ppermute x2, local copies, waits for them, and re-layouts, passed_along(): return lax.ppermute(block, axis, route)  9.72 us
  transfers between devices with their start and end apart: 7, of which 5 were waited for; matrix products, arithmetic and copies ran while one was open for 5% of the time, Pallas kernels for 0%

profile of v1, /device:TPU:1, one launch (start us, length us, event | category | flops | bytes accessed | tf_op | source)
XLA Modules:
  0.0 274.8 jit_solution(2315649546439868994)
XLA Ops:
  7.2 1.6 copy.28
  10.9 43.5 %all-gather.2.cloned.1.call-done = f32[4,2,64,512]{2,0,1,3:T(4,128)} async-done(((f32[4,2,64,32]{2,0,1,3:T(4,128)}), f32[4,2,64,512]{2,0,1,3:T(4,128)}) %all-gather.2.cloned.1.call-update) | async-done | bytes 1048592 | tf_op jit(solution)/shard_map/all_gather | solution.py:74
  54.4 1.7 fusion.128
  58.6 1.6 stack.56
  60.2 6.4 %all-to-all-start = ((f32[8,4,2,64,128]{4,3,2,1,0:T(8,128)}), f32[8,4,2,64,128]{4,3,2,1,0:T(8,128)S(1)}, u32[]{:S(2)}, u32[]{:S(2)}) async-start(f32[8,4,2,64,128]{4,3,2,1,0:T(8,128)} %stack.56), calls=%async_computation | async-start | bytes 4194304 | tf_op jit(solution)/shard_map/all_to_all | solution.py:19
  67.3 27.9 %all-to-all-done = f32[8,4,2,64,128]{4,3,2,1,0:T(8,128)S(1)} async-done(((f32[8,4,2,64,128]{4,3,2,1,0:T(8,128)}), f32[8,4,2,64,128]{4,3,2,1,0:T(8,128)S(1)}, u32[]{:S(2)}, u32[]{:S(2)}) %all-to-all-start) | async-done | bytes 2097184 | tf_op jit(solution)/shard_map/all_to_all | solution.py:19
  95.4 1.0 fusion.75
  96.5 1.0 fusion.74
  97.5 1.0 convolution_subtract_fusion
  98.5 1.1 subtract_reduce_fusion
  100.4 1.5 select_add_fusion
  101.8 32.6 %all-reduce.18.cloned.1.call-done = f32[2,256,128]{1,2,0:T(8,128)} async-done(((f32[2,256,128]{1,2,0:T(8,128)}), f32[2,256,128]{1,2,0:T(8,128)}) %all-reduce.18.cloned.1.call-update) | async-done | bytes 262160 | tf_op jit(solution)/shard_map/psum | solution.py:106
  134.4 1.1 copy.35
  135.5 1.1 pad_maximum_fusion.21
  136.6 4.6 %collective-permute-start = (f32[44,4,128]{2,1,0:T(4,128)S(1)}, f32[44,4,128]{2,1,0:T(4,128)S(1)}, u32[]{:S(2)}, u32[]{:S(2)}) collective-permute-start(f32[44,4,128]{2,1,0:T(4,128)S(1)} %get-tuple-element.134), channel_id=1, source_target_pairs={{16,0},{32,16},{48,32},{64,48},{80,64},{96,80},{112,96},{0,112},{1... | collective-permute-start | bytes 270344 | tf_op jit(solution)/shard_map/ppermute | solution.py:26
  141.3 1.6 collective-permute-done
  142.8 5.4 %collective-permute-done.1 = f32[44,4,128]{2,1,0:T(4,128)S(1)} collective-permute-done((f32[44,4,128]{2,1,0:T(4,128)S(1)}, f32[44,4,128]{2,1,0:T(4,128)S(1)}, u32[]{:S(2)}, u32[]{:S(2)}) %collective-permute-start.1) | collective-permute-done | bytes 90144 | tf_op jit(solution)/shard_map/ppermute | solution.py:26
  148.3 2.1 pad_maximum_fusion.1
  150.4 6.2 %slice_bitcast_fusion.1 = (f32[44,4,264]{1,2,0:T(8,128)}, f32[44,4,264]{1,2,0:T(8,128)}) fusion(f32[44,264,128]{2,1,0:T(8,128)S(1)} %pad_maximum_fusion.1), kind=kLoop, calls=%fused_computation.2 | loop fusion | bytes 743424 | tf_op jit(solution)/shard_map/transpose | solution.py:113
  156.6 5.5 %copy.36 = f32[44,4,264]{2,1,0:T(4,128)} copy(f32[44,4,264]{1,2,0:T(8,128)} %get-tuple-element.132) | data formatting | bytes 371712 | tf_op jit(solution)/shard_map/transpose | solution.py:113
  162.1 2.6 collective-permute-start.2
  164.7 5.5 %copy.38 = f32[44,4,264]{2,1,0:T(4,128)} copy(f32[44,4,264]{1,2,0:T(8,128)} %get-tuple-element.133) | data formatting | bytes 371712 | tf_op jit(solution)/shard_map/transpose | solution.py:114
  170.2 1.2 collective-permute-start.3
  171.3 4.8 %copy.37 = f32[44,4,264]{1,2,0:T(8,128)} copy(f32[44,4,264]{2,1,0:T(4,128)} %collective-permute-done.2) | data formatting | bytes 371712 | tf_op jit(solution)/shard_map/ppermute | solution.py:26
  176.2 4.9 %copy.39 = f32[44,4,264]{1,2,0:T(8,128)} copy(f32[44,4,264]{2,1,0:T(4,128)} %collective-permute-done.3) | data formatting | bytes 371712 | tf_op jit(solution)/shard_map/ppermute | solution.py:26
  181.1 7.5 %pad_maximum_fusion = f32[44,264,136]{2,1,0:T(8,128)S(1)} fusion(f32[44,264,4]{2,1,0:T(8,128)} %bitcast.132, f32[44,264,4]{2,1,0:T(8,128)} %bitcast.131, f32[44,4,128]{2,1,0:T(4,128)} %copy-done.14, f32[44,4,128]{2,1,0:T(4,128)S(1)} %collective-permute-done, f32[2,256,128]{2,1,0:T(8,128)S(1)} %copy.35, f32[6,256,128]{2,1,0:T(8,128)S(1)} %select_add_fusion, ...), kind=kLoop, calls=%fused_computation | loop fusion | flops 11058432 | bytes 12638208 | tf_op jit(solution)/shard_map/concatenate | solution.py:115
  189.7 2.5 copy-done.3
  193.0 1.2 slice.667
  194.5 2.7 fusion.9
  198.9 2.3 fusion.17
  201.2 1.0 slice.674
  202.4 1.0 slice.661
  203.4 1.2 slice.664
  204.7 1.6 slice.660
  206.4 1.6 slice.673
  208.0 1.3 slice.669
  210.0 4.1 %fusion.20 = (f32[6,264,136]{2,1,0:T(8,128)S(1)}, f32[6,264,136]{2,1,0:T(8,128)S(1)}, f32[6,264,136]{2,1,0:T(8,128)S(1)}) fusion(f32[6,264,136]{2,1,0:T(8,128)S(1)} %get-tuple-element.122, f32[6,264,136]{2,1,0:T(8,128)S(1)} %get-tuple-element.120, f32[6,1,136]{2,1,0:T(1,128)S(1)} %slice.659, f32[6,263,136]{2,1,0:T(8,128)S(1)} %slice.658, ...), kind=kLoop, calls=%fused_computation.42 | loop fusion | flops 4093056 | bytes 12638208 | tf_op jit(solution)/shard_map/sub | solution.py:141
  214.2 1.2 slice.662
  215.3 1.2 slice.671
  216.5 1.2 slice.689
  217.7 1.2 slice.676
  218.9 3.5 %fusion.35 = (f32[6,264,136]{2,1,0:T(8,128)S(1)}, f32[6,264,136]{2,1,0:T(8,128)S(1)}, f32[6,264,136]{2,1,0:T(8,128)S(1)}) fusion(f32[6,264,136]{2,1,0:T(8,128)S(1)} %get-tuple-element.120, f32[6,264,136]{2,1,0:T(8,128)S(1)} %get-tuple-element.147, f32[6,263,136]{2,1,0:T(8,128)S(1)} %bitcast.115, f32[6,1,136]{2,1,0:T(1,128)S(1)} %slice.677, ...), kind=kLoop, calls=%fused_computation.64 | loop fusion | flops 4093056 | bytes 13499904 | tf_op jit(solution)/shard_map/add | solution.py:143
  223.6 1.0 slice.683
  224.6 1.2 slice.686
  225.9 1.6 slice.682
  227.5 1.7 slice.695
  229.2 1.3 slice.691
  230.5 4.1 %fusion.38 = (f32[6,264,136]{2,1,0:T(8,128)S(1)}, f32[6,264,136]{2,1,0:T(8,128)S(1)}, f32[6,264,136]{2,1,0:T(8,128)S(1)}) fusion(f32[6,264,136]{2,1,0:T(8,128)S(1)} %get-tuple-element.147, f32[6,264,136]{2,1,0:T(8,128)S(1)} %get-tuple-element.118, f32[6,1,136]{2,1,0:T(1,128)S(1)} %slice.681, f32[6,263,136]{2,1,0:T(8,128)S(1)} %slice.680, ...), kind=kLoop, calls=%fused_computation.68 | loop fusion | flops 4093056 | bytes 12638208 | tf_op jit(solution)/shard_map/sub | solution.py:141
  234.7 1.4 slice.684
  236.1 1.2 slice.693
  237.3 1.2 slice.711
  238.5 1.2 slice.698
  240.4 3.5 %fusion.53 = (f32[6,264,136]{2,1,0:T(8,128)S(1)}, f32[6,264,136]{2,1,0:T(8,128)S(1)}, f32[6,264,136]{2,1,0:T(8,128)S(1)}) fusion(f32[6,264,136]{2,1,0:T(8,128)S(1)} %get-tuple-element.118, f32[6,264,136]{2,1,0:T(8,128)S(1)} %get-tuple-element.144, f32[6,263,136]{2,1,0:T(8,128)S(1)} %bitcast.117, f32[6,1,136]{2,1,0:T(1,128)S(1)} %slice.699, ...), kind=kLoop, calls=%fused_computation.90 | loop fusion | flops 4093056 | bytes 13499904 | tf_op jit(solution)/shard_map/add | solution.py:143
  245.6 1.3 copy-done.6
  246.9 2.3 fusion.56
  249.3 1.4 slice.706
  250.8 1.2 slice.728
  252.0 1.2 slice.721
  253.9 5.5 %fusion.59 = (f32[6,264,136]{2,1,0:T(8,128)}, f32[6,264,136]{2,1,0:T(8,128)}, f32[6,264,136]{2,1,0:T(8,128)}) fusion(f32[6,264,136]{2,1,0:T(8,128)S(1)} %get-tuple-element.117, f32[6,264,136]{2,1,0:T(8,128)S(1)} %get-tuple-element.141, f32[6,264,135]{2,1,0:T(8,128)S(1)} %bitcast.124, f32[6,264,1]{2,1,0:T(8,128)} %slice.706, ...), kind=kLoop, calls=%fused_computation.99 | loop fusion | flops 2585088 | bytes 10914816 | tf_op jit(solution)/shard_map/add | solution.py:142
  259.3 2.1 fusion.87
  261.4 1.6 slice_bitcast_fusion.9
  263.1 1.7 slice_bitcast_fusion.11
  264.8 1.6 pad_maximum_fusion.3
  266.4 1.6 pad_maximum_fusion.2
  (99 shorter events, 15.8 us)
Async XLA Ops:
  7.2 47.2 %all-gather.2.cloned.1.call-start = ((), (), s32[]{:S(2)}) async-start(), calls=%async_computation.1 | async-start | bytes 2228224 | tf_op jit(solution)/shard_map/all_gather | solution.py:74
  56.4 1.0 copy-start.13
  60.2 35.0 %all-to-all-start = ((f32[8,4,2,64,128]{4,3,2,1,0:T(8,128)}), f32[8,4,2,64,128]{4,3,2,1,0:T(8,128)S(1)}, u32[]{:S(2)}, u32[]{:S(2)}) async-start(f32[8,4,2,64,128]{4,3,2,1,0:T(8,128)} %stack.56), calls=%async_computation | async-start | bytes 4194304 | tf_op jit(solution)/shard_map/all_to_all | solution.py:19
  66.6 67.8 %all-reduce.18.cloned.1.call-start = ((), (), s32[]{:S(2)}) async-start(), calls=%async_computation.2 | async-start | bytes 524288 | tf_op jit(solution)/shard_map/psum | solution.py:106
  99.6 35.9 %copy-start.1 = (f32[3,6,256,128]{3,2,1,0:T(8,128)S(1)}, f32[3,6,256,128]{3,2,1,0:T(8,128)}, u32[]{:S(2)}) copy-start(f32[3,6,256,128]{3,2,1,0:T(8,128)} %param.25) | copy-start | bytes 7077892
  135.5 12.8 %copy-start.2 = (f32[3,6,256,128]{3,2,1,0:T(8,128)S(1)}, f32[3,6,256,128]{3,2,1,0:T(8,128)}, u32[]{:S(2)}) copy-start(f32[3,6,256,128]{3,2,1,0:T(8,128)} %param.24) | copy-start | bytes 7077892
  136.6 6.2 %collective-permute-start = (f32[44,4,128]{2,1,0:T(4,128)S(1)}, f32[44,4,128]{2,1,0:T(4,128)S(1)}, u32[]{:S(2)}, u32[]{:S(2)}) collective-permute-start(f32[44,4,128]{2,1,0:T(4,128)S(1)} %get-tuple-element.134), channel_id=1, source_target_pairs={{16,0},{32,16},{48,32},{64,48},{80,64},{96,80},{112,96},{0,112},{1... | collective-permute-start | bytes 270344 | tf_op jit(solution)/shard_map/ppermute | solution.py:26
  141.3 7.0 %collective-permute-start.1 = (f32[44,4,128]{2,1,0:T(4,128)S(1)}, f32[44,4,128]{2,1,0:T(4,128)S(1)}, u32[]{:S(2)}, u32[]{:S(2)}) collective-permute-start(f32[44,4,128]{2,1,0:T(4,128)S(1)} %get-tuple-element.135), channel_id=1, source_target_pairs={{112,0},{0,16},{16,32},{32,48},{48,64},{64,80},{80,96},{96,112},{1... | collective-permute-start | bytes 270344 | tf_op jit(solution)/shard_map/ppermute | solution.py:26
  148.3 2.1 copy-start.14
  162.1 9.2 %collective-permute-start.2 = (f32[44,4,264]{2,1,0:T(4,128)}, f32[44,4,264]{2,1,0:T(4,128)}, u32[]{:S(2)}, u32[]{:S(2)}) collective-permute-start(f32[44,4,264]{2,1,0:T(4,128)} %copy.36), channel_id=1, source_target_pairs={{1,0},{2,1},{3,2},{4,3},{5,4},{6,5},{7,6},{8,7},{9,8},{10,9},{11,1... | collective-permute-start | bytes 557576 | tf_op jit(solution)/shard_map/ppermute | solution.py:26
  170.2 6.0 %collective-permute-start.3 = (f32[44,4,264]{2,1,0:T(4,128)}, f32[44,4,264]{2,1,0:T(4,128)}, u32[]{:S(2)}, u32[]{:S(2)}) collective-permute-start(f32[44,4,264]{2,1,0:T(4,128)} %copy.38), channel_id=1, source_target_pairs={{15,0},{0,1},{1,2},{2,3},{3,4},{4,5},{5,6},{6,7},{7,8},{8,9},{9,10... | collective-permute-start | bytes 557576 | tf_op jit(solution)/shard_map/ppermute | solution.py:26
  188.6 55.4 %copy-start = (f32[44,264,136]{2,1,0:T(8,128)}, f32[44,264,136]{2,1,0:T(8,128)S(1)}, u32[]{:S(2)}) copy-start(f32[44,264,136]{2,1,0:T(8,128)S(1)} %pad_maximum_fusion) | copy-start | bytes 18957316
  188.8 3.4 %copy-start.3 = (f32[3,6,256,128]{3,2,1,0:T(8,128)S(1)}, f32[3,6,256,128]{3,2,1,0:T(8,128)}, u32[]{:S(2)}) copy-start(f32[3,6,256,128]{3,2,1,0:T(8,128)} %param.24) | copy-start | bytes 7077892
  188.8 3.4 %copy-start.15 = (f32[44,4,128]{2,1,0:T(4,128)S(1)}, f32[44,4,128]{2,1,0:T(4,128)}, u32[]{:S(2)}) copy-start(f32[44,4,128]{2,1,0:T(4,128)} %copy-done.14) | copy-start | bytes 270340
  197.2 1.2 copy-start.7
  197.5 1.4 copy-start.12
  208.0 2.0 copy-start.8
  234.6 2.7 copy-start.4
  238.5 1.9 copy-start.5
  245.5 1.4 copy-start.6
  249.2 1.5 copy-start.9
  252.0 1.9 copy-start.10
  261.4 1.6 copy-start.11
Sparse Core Ops, SparseCore 0:
  10.4 43.9 all-gather.1
  100.5 33.8 all-reduce.17
